TPU v7x, 32 devices: a whole 2x2x4 slice. The times are simulated.
32 devices in a mesh: section: 8 (over y, x, core), dp: 4 (over z).
Axes of the slice: x: 2, y: 2, z: 4, core: 2. Of those that a mesh axis runs over, the one named last changes fastest.
Arguments:
- activations: bfloat16 [2048, 8192], P('dp'), may hold values from -6 to 6
- cotangent: bfloat16 [2048, 8192], P('dp'), may hold values from -6 to 6
- gate_pre: bfloat16 [2048, 4096], P('dp', 'section'), may hold values from -6 to 6
- weights: bfloat16 [2, 8192, 4096], P(None, 'dp', 'section'), may hold values from -0.0625 to 0.0625
- holder_map: int32 [64, 8, 2], P('dp', 'section'), may hold values from 0 to 7, as said below
- master: float32 [8, 4, 48, 128, 512], P('section', 'dp'), may hold values from -0.0625 to 0.0625
- moment_one: float32 [8, 4, 48, 128, 512], P('section', 'dp'), may hold values from -80 to 80
- moment_two: float32 [8, 4, 48, 128, 512], P('section', 'dp'), may hold values from 102.4 to 4096
- adam_step: int32 [1], replicated, may hold values from 1 to 11
Outputs:
- passed_back: bfloat16 [2048, 8192], P('dp', 'section')
- new_weights: bfloat16 [2, 8192, 4096], P(None, 'dp', 'section')
Inputs may be any that keep to these rules, and one draw needn't show every extreme that they name: `holder_map`: every block of one device (32 of them) goes to holders of that device's dp index; one device sends to exactly 4 holder sections, exactly 8 blocks to each; each holder device receives at most 48 blocks from all sections, and in every dp column some holder receives exactly 48.
All inputs are finite; a program needn't handle non-finite values.
Results may differ from a plain program's by a relative error of at most 0.012.
Values may be sent and summed in bfloat16 or wider, within the bound.
A program may use at most 320 MiB of HBM per device.

v0:
```python
import jax
import jax.numpy as jnp
from jax import lax
from jax.sharding import PartitionSpec as P

learn_rate = 0.03
beta_one = 0.9
beta_two = 0.95
adam_eps = 1e-08
decay_rate = 0.1


def carried_in(shard, axis, combine, identity):
    devices, position = (lax.axis_size(axis), lax.axis_index(axis))
    everything = lax.all_gather(shard, axis)
    start = jnp.broadcast_to(jnp.asarray(identity, shard.dtype), shard.shape)

    def hop(k, before):
        reached = k < position
        new = combine(before, everything[k])
        return jnp.where(reached, new, before)

    return lax.fori_loop(0, devices, hop, start)


def adam_apply(gradient, weight_master, first_moment, second_moment, step_number):
    step_float = step_number.astype(jnp.float32)
    fix_one = 1.0 - jnp.power(jnp.float32(beta_one), step_float)
    fix_two = 1.0 - jnp.power(jnp.float32(beta_two), step_float)
    first_new = beta_one * first_moment + (1.0 - beta_one) * gradient
    second_new = beta_two * second_moment + (1.0 - beta_two) * gradient * gradient
    update = first_new / fix_one / (jnp.sqrt(second_new / fix_two) + adam_eps)
    return (weight_master * (1.0 - learn_rate * decay_rate) - learn_rate * update).astype(
        jnp.bfloat16
    )


def per_device(
    activations, cotangent, gate_pre, weights, holder_map, master, moment_one, moment_two, adam_step
):
    hidden_units = gate_pre.shape[1]
    row_count = weights.shape[1]
    sections = lax.axis_size("section")
    contract = (((1,), (1,)), ((), ()))
    over_tokens = (((0,), (0,)), ((), ()))
    gathered = lax.all_gather(weights, "dp", axis=1, tiled=True)
    up_full = gathered[0]
    lifted = jnp.dot(activations, up_full, preferred_element_type=jnp.float32)
    back_hidden = jnp.dot(cotangent, gathered[1], preferred_element_type=jnp.float32)
    gate_silu = jax.nn.silu(gate_pre.astype(jnp.float32))
    hidden = (gate_silu * lifted).astype(jnp.bfloat16)
    back_up = (back_hidden * gate_silu).astype(jnp.bfloat16)
    back_in = lax.dot_general(back_up, up_full, contract, preferred_element_type=jnp.float32)
    passed_back = lax.psum_scatter(
        back_in.astype(jnp.bfloat16), "section", scatter_dimension=1, tiled=True
    )
    summed = lax.psum_scatter(
        jnp.concatenate(
            [
                lax.dot_general(
                    activations, back_up, over_tokens, preferred_element_type=jnp.float32
                ),
                lax.dot_general(cotangent, hidden, over_tokens, preferred_element_type=jnp.float32),
            ],
            axis=1,
        ).astype(jnp.bfloat16),
        "dp",
        scatter_dimension=0,
        tiled=True,
    ).astype(jnp.float32)
    block_rows = master.shape[3]
    capacity = master.shape[2]
    row_blocks = row_count // block_rows
    per_dest = 4 * row_blocks // sections
    blocks = (
        summed.reshape(row_blocks, block_rows, 2, hidden_units)
        .transpose(0, 2, 1, 3)
        .reshape(-1, block_rows, hidden_units)
    )
    block_total = blocks.shape[0]
    owners = holder_map[:, 0, :].reshape(-1)
    section_ids = jnp.arange(sections, dtype=jnp.int32)
    choose = (owners[:, None] == section_ids[None, :]).astype(jnp.int32)
    ahead = jnp.cumsum(choose, axis=0) - choose
    order_in = jnp.sum(ahead * choose, axis=1)
    totals = jnp.sum(choose, axis=0)
    earlier = carried_in(
        totals,
        "section",
        lambda first_part, later_part: first_part + later_part,
        jnp.zeros_like(totals),
    )
    slot_of = order_in + jnp.sum(choose * earlier[None, :], axis=1).astype(jnp.int32)
    chosen = (owners[None, None, :] == section_ids[:, None, None]) & (
        order_in[None, None, :] == jnp.arange(per_dest, dtype=jnp.int32)[None, :, None]
    )
    present = jnp.any(chosen, axis=2)
    source_index = jnp.sum(
        jnp.where(chosen, jnp.arange(block_total, dtype=jnp.int32)[None, None, :], 0), axis=2
    )
    outgoing = jnp.take(blocks, source_index.reshape(-1), axis=0).reshape(
        sections, per_dest, block_rows, hidden_units
    )
    out_slot = jnp.where(
        present, jnp.sum(jnp.where(chosen, slot_of[None, None, :], 0), axis=2), capacity
    )
    step_number = adam_step[0]
    states = (master[0, 0], moment_one[0, 0], moment_two[0, 0])
    arrivals = lax.all_to_all(
        outgoing.astype(jnp.bfloat16), "section", split_axis=0, concat_axis=0, tiled=True
    ).astype(outgoing.dtype)
    item_slots = lax.all_to_all(out_slot, "section", split_axis=0, concat_axis=0, tiled=True)
    live = (item_slots < capacity).astype(jnp.float32).reshape(item_slots.shape + (1, 1))
    slot_index = jnp.minimum(item_slots, capacity - 1).reshape(-1)
    looked = [jnp.take(state, slot_index, axis=0).reshape(arrivals.shape) for state in states]
    updated = adam_apply(
        arrivals * live,
        looked[0] * live,
        looked[1] * live,
        looked[2] * live + (1.0 - live),
        step_number,
    )
    returned = lax.all_to_all(updated, "section", split_axis=0, concat_axis=0, tiled=True)
    new_blocks = jnp.take(
        returned.reshape(-1, block_rows, hidden_units), owners * per_dest + order_in, axis=0
    )
    new_rows = (
        new_blocks.reshape(row_blocks, 2, block_rows, hidden_units)
        .transpose(1, 0, 2, 3)
        .reshape(2, row_count, hidden_units)
    )
    return (passed_back, new_rows)


def solution(mesh):
    in_specs = (
        P("dp", None),
        P("dp", None),
        P("dp", "section"),
        P(None, "dp", "section"),
        P("dp", "section", None),
        P("section", "dp", None, None, None),
        P("section", "dp", None, None, None),
        P("section", "dp", None, None, None),
        P(),
    )
    out_specs = (P("dp", "section"), P(None, "dp", "section"))
    return jax.shard_map(
        per_device, mesh=mesh, in_specs=in_specs, out_specs=out_specs, check_vma=False
    )
```

profile of v0, /device:TPU:0, one launch (start us, length us, event | category | flops | bytes accessed | tf_op | source)
XLA Modules:
  0.0 910.2 jit_solution(6311418935512518231)
XLA Ops:
  7.2 0.7 all-gather.3.cloned.1.call-update
  7.9 291.1 %all-gather.3.cloned.1.call-done = bf16[2,8192,512]{2,1,0:T(8,128)(2,1)} async-done(((bf16[2,2048,512]{2,1,0:T(8,128)(2,1)}), bf16[2,8192,512]{2,1,0:T(8,128)(2,1)}) %all-gather.3.cloned.1.call-update) | async-done | bytes 16777232 | tf_op jit(solution)/shard_map/all_gather | solution.py:46
  299.1 10.4 %fusion.12 = bf16[512,512]{1,0:T(8,128)(2,1)S(1)} fusion(bf16[512,8192]{1,0:T(8,128)(2,1)} %param.14, bf16[2,8192,512]{2,1,0:T(8,128)(2,1)} %all-gather.3.cloned.1.call-done, bf16[512,512]{1,0:T(8,128)(2,1)} %param.15), kind=kOutput, calls=%fused_computation.35 | convolution fusion | flops 4296802304 | bytes 17825792 | tf_op jit(solution)/shard_map/dot_general | solution.py:49
  309.5 8.3 fusion.6
  317.8 7.1 fusion.13
  325.0 8.2 fusion.7
  333.2 6.7 pad_maximum_fusion
  339.9 0.6 copy-done.1
  340.7 0.6 dynamic-slice
  342.3 7.9 all-reduce
  350.4 0.3 while.14
  351.2 0.4 fusion.18
  351.6 0.6 broadcast_select_fusion.5
  352.2 3.5 all-to-all-start
  355.8 262.8 %reduce-scatter.5.cloned.1.call-done = bf16[2048,1024]{0,1:T(8,128)(2,1)} async-done(((bf16[8192,1024]{0,1:T(8,128)(2,1)}), bf16[2048,1024]{0,1:T(8,128)(2,1)}) %reduce-scatter.5.cloned.1.call-update) | async-done | bytes 4194320 | tf_op jit(solution)/shard_map/reduce_scatter | solution.py:57
  618.6 5.6 copy.41
  624.2 7.6 copy.38
  631.8 7.6 gather_fusion
  639.4 10.4 %select_convert_fusion = bf16[8,8,128,512]{3,2,1,0:T(8,128)(2,1)} fusion(bf16[8,8,128,512]{3,2,1,0:T(8,128)(2,1)} %bitcast.83, pred[8,8]{1,0:T(8,128)(4,1)S(1)} %compare_and_fusion), kind=kLoop, calls=%fused_computation.16 | loop fusion | flops 4194304 | bytes 16777280 | tf_op jit(solution)/shard_map/convert_element_type | solution.py:110
  649.8 4.9 all-to-all-start.1
  655.9 13.0 %gather_fusion.4 = f32[64,128,512]{2,1,0:T(8,128)} fusion(f32[48,128,512]{2,1,0:T(8,128)} %bitcast.84, s32[1024]{0:T(1024)S(1)} %pad_clamp_fusion.2), kind=kCustom, calls=%fused_computation.2.clone | custom fusion | bytes 33554688 | tf_op jit(solution)/shard_map/jit(_take)/gather | solution.py:115
  668.9 13.0 %gather_fusion.3 = f32[64,128,512]{2,1,0:T(8,128)} fusion(f32[48,128,512]{2,1,0:T(8,128)} %bitcast.85, s32[1024]{0:T(1024)S(1)} %pad_clamp_fusion.2), kind=kCustom, calls=%fused_computation.1.clone | custom fusion | bytes 33554688 | tf_op jit(solution)/shard_map/jit(_take)/gather | solution.py:115
  681.8 12.9 %gather_fusion.2 = f32[64,128,512]{2,1,0:T(8,128)} fusion(f32[48,128,512]{2,1,0:T(8,128)} %bitcast.86, s32[1024]{0:T(1024)S(1)} %pad_clamp_fusion.2), kind=kCustom, calls=%fused_computation.clone | custom fusion | bytes 33554688 | tf_op jit(solution)/shard_map/jit(_take)/gather | solution.py:115
  694.8 33.9 %broadcast_select_fusion.3 = (f32[64,128,512]{2,1,0:T(8,128)}, f32[64,128,512]{2,1,0:T(8,128)}, f32[64,128,512]{2,1,0:T(8,128)}) fusion(f32[64,128,512]{2,1,0:T(8,128)} %gather_fusion.3, pred[64]{0:T(512)(128)(4,1)S(1)} %compare_and_fusion.1, f32[64,128,512]{2,1,0:T(8,128)} %gather_fusion.4, f32[64,128,512]{2,1,0:T(8,128)} %gather_fusion.2), kind=kLoop, calls=%fused_computation.26 | loop fusion | flops 12582912 | bytes 100663360 | tf_op jit(solution)/shard_map/jit(_take)/select_n | solution.py:115
  728.7 10.1 %convolution_convert_fusion.2 = bf16[512,8192]{1,0:T(8,128)(2,1)} fusion(bf16[512,512]{1,0:T(8,128)(2,1)S(1)} %fusion.12, bf16[2,8192,512]{2,1,0:T(8,128)(2,1)} %all-gather.3.cloned.1.call-done), kind=kOutput, calls=%fused_computation.19 | convolution fusion | flops 4299161600 | bytes 17301504 | tf_op jit(solution)/shard_map/dot_general | solution.py:53
  738.8 10.1 %all-to-all-done.1 = bf16[8,8,128,512]{3,2,1,0:T(8,128)(2,1)} async-done(((bf16[8,8,128,512]{3,2,1,0:T(8,128)(2,1)}), bf16[8,8,128,512]{3,2,1,0:T(8,128)(2,1)}, u32[]{:S(2)}, u32[]{:S(2)}) %all-to-all-start.1) | async-done | bytes 8388640 | tf_op jit(solution)/shard_map/all_to_all | solution.py:109
  748.8 28.3 %subtract_convert_fusion = bf16[8,8,128,512]{3,2,1,0:T(8,128)(2,1)} fusion(f32[8,8,128,512]{3,2,1,0:T(8,128)} %bitcast.81, f32[8,8,128,512]{3,2,1,0:T(8,128)} %bitcast.80, bf16[8,8,128,512]{3,2,1,0:T(8,128)(2,1)} %all-to-all-done.1, f32[8,8,128,512]{3,2,1,0:T(8,128)} %bitcast.79, f32[]{:T(128)} %bitcast.21, f32[8,8]{1,0:T(8,128)S(1)} %broadcast_subtract_fusion, ...), kind=kLoop, calls=%fused_computation.15 | loop fusion | flops 88080384 | bytes 67109384 | tf_op jit(solution)/shard_map/convert_element_type | solution.py:33
  777.1 5.0 all-to-all-start.2
  782.5 109.8 %all-to-all-done.2 = bf16[8,8,128,512]{3,2,1,0:T(8,128)(2,1)} async-done(((bf16[8,8,128,512]{3,2,1,0:T(8,128)(2,1)}), bf16[8,8,128,512]{3,2,1,0:T(8,128)(2,1)}, u32[]{:S(2)}, u32[]{:S(2)}) %all-to-all-start.2) | async-done | bytes 8388640 | tf_op jit(solution)/shard_map/all_to_all | solution.py:123
  892.4 6.2 gather_fusion.1
  898.6 2.6 select_bitcast_fusion
  901.2 2.5 copy.40
  (56 shorter events, 2.4 us)
Async XLA Ops:
  7.2 291.9 %all-gather.3.cloned.1.call-start = ((), (), s32[]{:S(2)}) async-start(), calls=%async_computation.5 | async-start | bytes 20971520 | tf_op jit(solution)/shard_map/all_gather | solution.py:46
  7.9 610.7 %reduce-scatter.5.cloned.1.call-start = ((), (), s32[]{:S(2)}) async-start(), calls=%async_computation.7 | async-start | bytes 20971520 | tf_op jit(solution)/shard_map/reduce_scatter | solution.py:57
  309.5 8.4 copy-start
  309.5 8.4 copy-start.2
  339.9 0.7 copy-start.1
  339.9 0.9 copy-start.3
  352.2 297.7 %all-to-all-start = ((s32[8,1,8]{2,1,0:T(1,128)}), s32[8,1,8]{2,1,0:T(1,128)S(1)}, u32[]{:S(2)}, u32[]{:S(2)}) async-start(s32[8,1,8]{2,1,0:T(1,128)} %bitcast.5), calls=%async_computation.1 | async-start | bytes 8192 | tf_op jit(solution)/shard_map/all_to_all | solution.py:112
  649.8 99.0 %all-to-all-start.1 = ((bf16[8,8,128,512]{3,2,1,0:T(8,128)(2,1)}), bf16[8,8,128,512]{3,2,1,0:T(8,128)(2,1)}, u32[]{:S(2)}, u32[]{:S(2)}) async-start(bf16[8,8,128,512]{3,2,1,0:T(8,128)(2,1)} %select_convert_fusion), calls=%async_computation.3 | async-start | bytes 16777216 | tf_op jit(solution)/shard_map/all_to_all | solution.py:109
  654.8 248.9 %reduce-scatter.3.cloned.1.call-start = ((), (), s32[]{:S(2)}) async-start(), calls=%async_computation.6 | async-start | bytes 9437184 | tf_op jit(solution)/shard_map/reduce_scatter | solution.py:54
  777.1 115.3 %all-to-all-start.2 = ((bf16[8,8,128,512]{3,2,1,0:T(8,128)(2,1)}), bf16[8,8,128,512]{3,2,1,0:T(8,128)(2,1)}, u32[]{:S(2)}, u32[]{:S(2)}) async-start(bf16[8,8,128,512]{3,2,1,0:T(8,128)(2,1)} %subtract_convert_fusion), calls=%async_computation.4 | async-start | bytes 16777216 | tf_op jit(solution)/shard_map/all_to_all | solution.py:123
Sparse Core Ops, SparseCore 0:
  9.6 289.4 all-gather.2
  340.0 278.5 reduce-scatter.4
  738.9 121.2 reduce-scatter.2
where the time goes:
time: 911 us; the launch traced here: 910 us
  waiting for transfers between devices  675 us (74%)
  other arithmetic  83.7 us (9%)
  local copies, waits for them, and re-layouts  70.7 us (8%)
  matrix products  44.1 us (5%)
  between operations  15.3 us (2%)
  starting transfers between devices  13.7 us (2%)
    all_gather x1, waiting for transfers between devices, per_device(): gathered = lax.all_gather(weights, 'dp', axis=1, tiled=True)  291 us
    reduce_scatter x1, waiting for transfers between devices, per_device(): lax.psum_scatter(jnp.concatenate([lax.dot_general(activations, back_up, o...  263 us
    all_to_all x1, waiting for transfers between devices, per_device(): lax.all_to_all(updated, 'section', split_axis=0, concat_axis=0, tiled=True)  110 us
    gather x3, local copies, waits for them, and re-layouts, per_device(): jnp.take(state, slot_index, axis=0).reshape(arrivals.shape)  38.9 us
    select_n x2, other arithmetic, per_device(): jnp.take(state, slot_index, axis=0).reshape(arrivals.shape)  33.9 us
    convert_element_type x1, other arithmetic, adam_apply(): (weight_master * (1.0 - learn_rate * decay_rate) - learn_rate * update).a...  28.3 us
  transfers between devices with their start and end apart: 6, of which 4 were waited for; matrix products, arithmetic and copies ran while one was open for 17% of the time, Pallas kernels for 0%

commit v1 on v0

--- a/solution.py
+++ b/solution.py
@@ -43,7 +43,12 @@
     sections = lax.axis_size("section")
     contract = (((1,), (1,)), ((), ()))
     over_tokens = (((0,), (0,)), ((), ()))
-    gathered = lax.all_gather(weights, "dp", axis=1, tiled=True)
+    ring = [weights]
+    for hop_ in range(3):
+        ring.append(lax.ppermute(ring[-1], "dp", [(dev, (dev + 1) % 4) for dev in range(4)]))
+    gathered = jnp.roll(
+        jnp.concatenate(ring[::-1], axis=1), (lax.axis_index("dp") + 1) * ring[0].shape[1], axis=1
+    )
     up_full = gathered[0]
     lifted = jnp.dot(activations, up_full, preferred_element_type=jnp.float32)
     back_hidden = jnp.dot(cotangent, gathered[1], preferred_element_type=jnp.float32)

time: 911 us -> 936 us (1.027)
  local copies, waits for them, and re-layouts: 70.7 us -> 102 us
  waiting for transfers between devices: 675 us -> 660 us
    all_gather x1 -> x0, waiting for transfers between devices: 291 us -> none  [per_device(): gathered = lax.all_gather(weights, 'dp', axis=1, tiled=True)]
    ppermute x0 -> x3, waiting for transfers between devices: none -> 278 us  [per_device(): lax.ppermute(ring[-1], 'dp', [(dev, (dev + 1) % 4) for dev in range(4)])]
    unnamed x13 -> x27, local copies, waits for them, and re-layouts: 7.18 us -> 35.7 us
  transfers between devices with their start and end apart: 6 -> 8, of which waited for: 4 -> 7; matrix products, arithmetic and copies ran while one was open for 17% -> 14% of each run, Pallas kernels for 0% -> 0%
where the time goes in v1:
time: 936 us; the launch traced here: 929 us
  waiting for transfers between devices  660 us (71%)
  local copies, waits for them, and re-layouts  102 us (11%)
  other arithmetic  83.8 us (9%)
  matrix products  41.5 us (4%)
  between operations  17.3 us (2%)
  starting transfers between devices  16.9 us (2%)
    ppermute x3, waiting for transfers between devices, per_device(): lax.ppermute(ring[-1], 'dp', [(dev, (dev + 1) % 4) for dev in range(4)])  278 us
    reduce_scatter x1, waiting for transfers between devices, per_device(): lax.psum_scatter(jnp.concatenate([lax.dot_general(activations, back_up, o...  258 us
    all_to_all x1, waiting for transfers between devices, per_device(): lax.all_to_all(updated, 'section', split_axis=0, concat_axis=0, tiled=True)  110 us
    gather x3, local copies, waits for them, and re-layouts, per_device(): jnp.take(state, slot_index, axis=0).reshape(arrivals.shape)  39.1 us
    unnamed x27, local copies, waits for them, and re-layouts  35.7 us
    select_n x2, other arithmetic, per_device(): jnp.take(state, slot_index, axis=0).reshape(arrivals.shape)  33.9 us
    convert_element_type x1, other arithmetic, adam_apply(): (weight_master * (1.0 - learn_rate * decay_rate) - learn_rate * update).a...  28.4 us
  transfers between devices with their start and end apart: 8, of which 7 were waited for; matrix products, arithmetic and copies ran while one was open for 14% of the time, Pallas kernels for 0%

profile of v1, /device:TPU:0, one launch (start us, length us, event | category | flops | bytes accessed | tf_op | source)
XLA Modules:
  0.0 929.4 jit_solution(7938572358577447032)
XLA Ops:
  8.0 3.1 collective-permute-start
  11.1 92.8 %collective-permute-done = bf16[2,2048,512]{2,1,0:T(8,128)(2,1)S(1)} collective-permute-done((bf16[2,2048,512]{2,1,0:T(8,128)(2,1)}, bf16[2,2048,512]{2,1,0:T(8,128)(2,1)S(1)}, u32[]{:S(2)}, u32[]{:S(2)}) %collective-permute-start) | collective-permute-done | bytes 4194336 | tf_op jit(solution)/shard_map/ppermute | solution.py:48
  105.9 93.7 %collective-permute-done.1 = bf16[2,2048,512]{2,1,0:T(8,128)(2,1)} collective-permute-done((bf16[2,2048,512]{2,1,0:T(8,128)(2,1)S(1)}, bf16[2,2048,512]{2,1,0:T(8,128)(2,1)}, u32[]{:S(2)}, u32[]{:S(2)}) %collective-permute-start.1) | collective-permute-done | bytes 4194336 | tf_op jit(solution)/shard_map/ppermute | solution.py:48
  200.9 91.7 %collective-permute-done.2 = bf16[2,2048,512]{2,1,0:T(8,128)(2,1)} collective-permute-done((bf16[2,2048,512]{2,1,0:T(8,128)(2,1)}, bf16[2,2048,512]{2,1,0:T(8,128)(2,1)}, u32[]{:S(2)}, u32[]{:S(2)}) %collective-permute-start.2) | collective-permute-done | bytes 4194336 | tf_op jit(solution)/shard_map/ppermute | solution.py:48
  292.6 4.6 constant_dynamic-update-slice_fusion.7
  297.1 4.4 constant_dynamic-update-slice_fusion.6
  306.3 4.7 constant_dynamic-update-slice_fusion.3
  310.9 4.4 constant_dynamic-update-slice_fusion.2
  320.2 10.8 %fusion.15 = bf16[512,512]{0,1:T(8,128)(2,1)S(1)} fusion(bf16[512,8192]{1,0:T(8,128)(2,1)} %param.13, bf16[2,16384,512]{2,1,0:T(8,128)(2,1)} %constant_dynamic-update-slice_fusion, s32[]{:T(128)S(6)} %select_n.106, bf16[512,512]{0,1:T(8,128)(2,1)S(1)} %copy.37), kind=kOutput, calls=%fused_computation.38 | convolution fusion | flops 4296802304 | bytes 17825796 | tf_op jit(solution)/shard_map/dot_general | solution.py:53
  331.0 7.5 fusion.14
  338.6 4.7 fusion.7
  343.3 8.1 fusion.6
  351.4 6.7 pad_maximum_fusion
  360.4 7.5 all-reduce
  369.9 3.8 all-to-all-start
  373.8 4.4 all-to-all-done
  378.4 258.0 %reduce-scatter.5.cloned.1.call-done = bf16[2048,1024]{0,1:T(8,128)(2,1)} async-done(((bf16[8192,1024]{0,1:T(8,128)(2,1)}), bf16[2048,1024]{0,1:T(8,128)(2,1)}) %reduce-scatter.5.cloned.1.call-update) | async-done | bytes 4194320 | tf_op jit(solution)/shard_map/reduce_scatter | solution.py:62
  636.4 5.6 copy.46
  642.0 7.6 copy.43
  649.6 7.6 gather_fusion
  657.2 10.4 %select_convert_fusion = bf16[8,8,128,512]{3,2,1,0:T(8,128)(2,1)} fusion(bf16[8,8,128,512]{3,2,1,0:T(8,128)(2,1)} %bitcast.99, pred[8,8]{1,0:T(8,128)(4,1)S(1)} %compare_and_fusion), kind=kLoop, calls=%fused_computation.16 | loop fusion | flops 4194304 | bytes 16777280 | tf_op jit(solution)/shard_map/convert_element_type | solution.py:115
  667.6 4.9 all-to-all-start.1
  673.4 13.2 %gather_fusion.3 = f32[64,128,512]{2,1,0:T(8,128)} fusion(f32[48,128,512]{2,1,0:T(8,128)} %bitcast.100, s32[1024]{0:T(1024)S(1)} %get-tuple-element.114), kind=kCustom, calls=%fused_computation.1.clone | custom fusion | bytes 33554688 | tf_op jit(solution)/shard_map/jit(_take)/gather | solution.py:120
  686.6 13.0 %gather_fusion.4 = f32[64,128,512]{2,1,0:T(8,128)} fusion(f32[48,128,512]{2,1,0:T(8,128)} %bitcast.101, s32[1024]{0:T(1024)S(1)} %get-tuple-element.114), kind=kCustom, calls=%fused_computation.2.clone | custom fusion | bytes 33554688 | tf_op jit(solution)/shard_map/jit(_take)/gather | solution.py:120
  699.5 12.9 %gather_fusion.2 = f32[64,128,512]{2,1,0:T(8,128)} fusion(f32[48,128,512]{2,1,0:T(8,128)} %bitcast.102, s32[1024]{0:T(1024)S(1)} %get-tuple-element.114), kind=kCustom, calls=%fused_computation.clone | custom fusion | bytes 33554688 | tf_op jit(solution)/shard_map/jit(_take)/gather | solution.py:120
  712.5 33.9 %broadcast_select_fusion.3 = (f32[64,128,512]{2,1,0:T(8,128)}, f32[64,128,512]{2,1,0:T(8,128)}, f32[64,128,512]{2,1,0:T(8,128)}) fusion(f32[64,128,512]{2,1,0:T(8,128)} %gather_fusion.3, pred[64]{0:T(512)(128)(4,1)S(1)} %compare_and_fusion.1, f32[64,128,512]{2,1,0:T(8,128)} %gather_fusion.4, f32[64,128,512]{2,1,0:T(8,128)} %gather_fusion.2), kind=kLoop, calls=%fused_computation.26 | loop fusion | flops 12582912 | bytes 100663360 | tf_op jit(solution)/shard_map/jit(_take)/select_n | solution.py:120
  746.4 10.3 %convolution_convert_fusion.2 = bf16[512,8192]{1,0:T(8,128)(2,1)} fusion(bf16[512,512]{0,1:T(8,128)(2,1)S(1)} %fusion.14, bf16[2,16384,512]{2,1,0:T(8,128)(2,1)} %constant_dynamic-update-slice_fusion, s32[]{:T(128)S(6)} %select_n.106), kind=kOutput, calls=%fused_computation.19 | convolution fusion | flops 4299161600 | bytes 17301508 | tf_op jit(solution)/shard_map/dot_general | solution.py:58
  756.7 10.0 %all-to-all-done.1 = bf16[8,8,128,512]{3,2,1,0:T(8,128)(2,1)} async-done(((bf16[8,8,128,512]{3,2,1,0:T(8,128)(2,1)}), bf16[8,8,128,512]{3,2,1,0:T(8,128)(2,1)}, u32[]{:S(2)}, u32[]{:S(2)}) %all-to-all-start.1) | async-done | bytes 8388640 | tf_op jit(solution)/shard_map/all_to_all | solution.py:114
  766.7 28.4 %subtract_convert_fusion = bf16[8,8,128,512]{3,2,1,0:T(8,128)(2,1)} fusion(f32[8,8,128,512]{3,2,1,0:T(8,128)} %bitcast.97, f32[8,8,128,512]{3,2,1,0:T(8,128)} %bitcast.96, bf16[8,8,128,512]{3,2,1,0:T(8,128)(2,1)} %all-to-all-done.1, f32[8,8,128,512]{3,2,1,0:T(8,128)} %bitcast.95, f32[]{:T(128)} %bitcast.23, f32[8,8]{1,0:T(8,128)S(1)} %broadcast_subtract_fusion, ...), kind=kLoop, calls=%fused_computation.15 | loop fusion | flops 88080384 | bytes 67109384 | tf_op jit(solution)/shard_map/convert_element_type | solution.py:33
  795.1 5.0 all-to-all-start.2
  800.6 109.9 %all-to-all-done.2 = bf16[8,8,128,512]{3,2,1,0:T(8,128)(2,1)} async-done(((bf16[8,8,128,512]{3,2,1,0:T(8,128)(2,1)}), bf16[8,8,128,512]{3,2,1,0:T(8,128)(2,1)}, u32[]{:S(2)}, u32[]{:S(2)}) %all-to-all-start.2) | async-done | bytes 8388640 | tf_op jit(solution)/shard_map/all_to_all | solution.py:128
  910.4 6.2 gather_fusion.1
  (74 shorter events, 22.5 us)
Async XLA Ops:
  8.0 628.4 %reduce-scatter.5.cloned.1.call-start = ((), (), s32[]{:S(2)}) async-start(), calls=%async_computation.6 | async-start | bytes 20971520 | tf_op jit(solution)/shard_map/reduce_scatter | solution.py:62
  8.0 95.9 %collective-permute-start = (bf16[2,2048,512]{2,1,0:T(8,128)(2,1)}, bf16[2,2048,512]{2,1,0:T(8,128)(2,1)S(1)}, u32[]{:S(2)}, u32[]{:S(2)}) collective-permute-start(bf16[2,2048,512]{2,1,0:T(8,128)(2,1)} %param.16), channel_id=1, source_target_pairs={{0,1},{1,2},{2,3},{3,0},{4,5},{5,6},{6,7},{7,4},{8,9},{9,10},{10,1... | collective-permute-start | bytes 12582920 | tf_op jit(solution)/shard_map/ppermute | solution.py:48
  103.9 2.0 copy-start.1
  105.9 93.7 %collective-permute-start.1 = (bf16[2,2048,512]{2,1,0:T(8,128)(2,1)S(1)}, bf16[2,2048,512]{2,1,0:T(8,128)(2,1)}, u32[]{:S(2)}, u32[]{:S(2)}) collective-permute-start(bf16[2,2048,512]{2,1,0:T(8,128)(2,1)S(1)} %collective-permute-done), channel_id=1, source_target_pairs={{0,1},{1,2},{2,3},{3,0},{4,5},{5,6},{6,7},{7,4},{8,9},{9,10},{10,1... | collective-permute-start | bytes 12582920 | tf_op jit(solution)/shard_map/ppermute | solution.py:48
  199.6 93.0 %collective-permute-start.2 = (bf16[2,2048,512]{2,1,0:T(8,128)(2,1)}, bf16[2,2048,512]{2,1,0:T(8,128)(2,1)}, u32[]{:S(2)}, u32[]{:S(2)}) collective-permute-start(bf16[2,2048,512]{2,1,0:T(8,128)(2,1)} %collective-permute-done.1), channel_id=1, source_target_pairs={{0,1},{1,2},{2,3},{3,0},{4,5},{5,6},{6,7},{7,4},{8,9},{9,10},{10,1... | collective-permute-start | bytes 12582920 | tf_op jit(solution)/shard_map/ppermute | solution.py:48
  200.9 100.7 %copy-start.2 = (bf16[2,2048,512]{2,1,0:T(8,128)(2,1)S(1)}, bf16[2,2048,512]{2,1,0:T(8,128)(2,1)}, u32[]{:S(2)}) copy-start(bf16[2,2048,512]{2,1,0:T(8,128)(2,1)} %copy-done.1) | copy-start | bytes 12582916
  200.9 103.0 %copy-start = (bf16[2,2048,512]{2,1,0:T(8,128)(2,1)S(1)}, bf16[2,2048,512]{2,1,0:T(8,128)(2,1)}, u32[]{:S(2)}) copy-start(bf16[2,2048,512]{2,1,0:T(8,128)(2,1)} %param.16) | copy-start | bytes 12582916
  317.8 13.2 %slice-start = ((s8[8388608]{0:T(1024)(128)(4,1)}), s8[4194304]{0:T(1024)(128)(4,1)S(1)}, s32[]{:S(2)}) async-start(s8[8388608]{0:T(1024)(128)(4,1)} %bitcast.109), calls=%async_computation.7 | async-start | bytes 8388608
  320.2 10.8 %slice-start.1 = ((s8[8388608]{0:T(1024)(128)(4,1)}), s8[4194304]{0:T(1024)(128)(4,1)S(1)}, s32[]{:S(2)}) async-start(s8[8388608]{0:T(1024)(128)(4,1)} %bitcast.109), calls=%async_computation.8 | async-start | bytes 8388608
  358.1 0.7 copy-start.3
  358.1 0.9 copy-start.4
  369.9 8.3 all-to-all-start
  667.6 99.0 %all-to-all-start.1 = ((bf16[8,8,128,512]{3,2,1,0:T(8,128)(2,1)}), bf16[8,8,128,512]{3,2,1,0:T(8,128)(2,1)}, u32[]{:S(2)}, u32[]{:S(2)}) async-start(bf16[8,8,128,512]{3,2,1,0:T(8,128)(2,1)} %select_convert_fusion), calls=%async_computation.3 | async-start | bytes 16777216 | tf_op jit(solution)/shard_map/all_to_all | solution.py:114
  672.6 249.2 %reduce-scatter.3.cloned.1.call-start = ((), (), s32[]{:S(2)}) async-start(), calls=%async_computation.5 | async-start | bytes 9437184 | tf_op jit(solution)/shard_map/reduce_scatter | solution.py:59
  795.1 115.3 %all-to-all-start.2 = ((bf16[8,8,128,512]{3,2,1,0:T(8,128)(2,1)}), bf16[8,8,128,512]{3,2,1,0:T(8,128)(2,1)}, u32[]{:S(2)}, u32[]{:S(2)}) async-start(bf16[8,8,128,512]{3,2,1,0:T(8,128)(2,1)} %subtract_convert_fusion), calls=%async_computation.4 | async-start | bytes 16777216 | tf_op jit(solution)/shard_map/all_to_all | solution.py:128
Sparse Core Ops, SparseCore 0:
  358.2 278.1 reduce-scatter.4
Sparse Core Ops, SparseCore 1:
  756.8 121.3 reduce-scatter.2
